TPU v7x, 512 devices: a whole 4x4x16 slice. The times are simulated.
512 devices in a mesh: ctx: 16 (over z_lo, core), head: 32 (over z_hi, y, x).
Axes of the slice: x: 4, y: 4, z: 16 (z_hi: 2, z_lo: 8; z = z_hi * 8 + z_lo), core: 2. Of those that a mesh axis runs over, the one named last changes fastest.
Arguments:
- tokens: bfloat16 [4096, 4096], P('ctx', 'head'), may hold values from -6 to 6
- qkv_weight: bfloat16 [4096, 3, 4096], P(None, None, 'head'), may hold values from -0.09375 to 0.09375
- out_weight: bfloat16 [4096, 4096], P('head'), may hold values from -1 to 1
- signs: int32 [32, 2, 128], P('head'), may hold values from 0 to 1
- rows: int32 [32, 2, 64], P('head'), may hold values from 0 to 127
Outputs:
- mixed: bfloat16 [4096, 4096], P('ctx', 'head')
Inputs may be any that keep to these rules, and one draw needn't show every extreme that they name: `signs`: each sign bit s gives the sign 2 s - 1. `rows`: rows are drawn with repetition.
All inputs are finite; a program needn't handle non-finite values.
Results may differ from a plain program's by a relative error of at most 0.025.
Values may be sent and summed in bfloat16 or wider, within the bound.
A program may use at most 128 MiB of HBM per device.

v0:
```python
import math

import jax
import jax.numpy as jnp
from jax import lax
from jax.sharding import PartitionSpec as P

BLOCK = 256


score_scale = 2.0


def prefix(value, axis, join, neutral):
    place = lax.axis_index(axis)
    gathered = jax.tree.map(
        lambda a, kind: lax.all_gather(a.astype(kind), axis), value, (jnp.bfloat16, jnp.bfloat16)
    )
    state = jax.tree.map(lambda a, e: jnp.zeros_like(a) + jnp.asarray(e, a.dtype), value, neutral)

    def one(hop, state):
        return join(
            state,
            jax.tree.map(
                lambda a, own: lax.dynamic_index_in_dim(a, hop, 0, False).astype(own.dtype),
                gathered,
                value,
            ),
        )

    return lax.fori_loop(0, place, one, state)


def hadamard_table(size_hd):
    row_index = jnp.arange(size_hd, dtype=jnp.int32)[:, None]
    col_index = jnp.arange(size_hd, dtype=jnp.int32)[None, :]
    common = jnp.bitwise_and(row_index, col_index)
    parity = jnp.zeros((size_hd, size_hd), jnp.int32)
    for bit_place in range(size_hd.bit_length() - 1):
        parity = parity + jnp.bitwise_and(jnp.right_shift(common, bit_place), 1)
    return 1.0 - 2.0 * jnp.bitwise_and(parity, 1).astype(jnp.float32)


def sketch_matrix(signs, rows):
    size_hd = signs.shape[-1]
    hadamard = hadamard_table(size_hd)
    selector = (jnp.arange(size_hd, dtype=jnp.int32)[:, None] == rows[..., None, :]).astype(
        jnp.float32
    )
    columns = jnp.einsum("de,kief->kidf", hadamard, selector, precision=lax.Precision.HIGHEST)
    signed = (2 * signs - 1).astype(jnp.float32)
    return (signed[..., None] * columns).astype(jnp.bfloat16)


def normalize(raw_rows):
    scale_rows = lax.rsqrt(jnp.mean(raw_rows * raw_rows, axis=-1, keepdims=True) + 1e-06)
    return (raw_rows * scale_rows).astype(jnp.bfloat16)


def features(normed, sketch):
    size_hd = sketch.shape[2]
    size_m = sketch.shape[3]
    branches = jnp.einsum("tkd,kidm->tkim", normed, sketch, preferred_element_type=jnp.float32)
    factor = score_scale * score_scale / (size_hd * math.sqrt(size_m))
    sketched = factor * branches[:, :, 0, :] * branches[:, :, 1, :]
    squared = sketched[:, :, :, None] * sketched[:, :, None, :]
    return squared.reshape(sketched.shape[0], sketched.shape[1], size_m * size_m).astype(
        jnp.bfloat16
    )


def add_pair(earlier, later):
    return (earlier[0] + later[0], earlier[1] + later[1])


def shards(tokens, qkv_weight, out_weight, signs, rows):
    length = tokens.shape[0]
    local_heads = signs.shape[0]
    size_hd = signs.shape[2]
    model_width = qkv_weight.shape[0]
    flat_weight = qkv_weight.reshape(model_width, 3 * local_heads * size_hd)
    projected = jnp.dot(
        lax.all_gather(tokens, "head", axis=1, tiled=True),
        flat_weight,
        preferred_element_type=jnp.float32,
    )
    projected = projected.reshape(length, 3, local_heads, size_hd)
    normed_queries = normalize(projected[:, 0])
    normed_keys = normalize(projected[:, 1])
    values = projected[:, 2].astype(jnp.bfloat16)
    sketch = sketch_matrix(signs, rows)
    query_feats = features(normed_queries, sketch)
    key_feats = features(normed_keys, sketch)
    feat_width = query_feats.shape[2]
    nblocks = length // BLOCK
    qf = query_feats.reshape(nblocks, BLOCK, local_heads, feat_width)
    kf = key_feats.reshape(nblocks, BLOCK, local_heads, feat_width)
    vbk = values.reshape(nblocks, BLOCK, local_heads, size_hd)
    block_states = jnp.einsum("btkf,btkd->bkfd", kf, vbk, preferred_element_type=jnp.float32)
    block_sums = jnp.sum(kf, axis=1, dtype=jnp.float32)
    state_zero = jnp.zeros((local_heads, feat_width, size_hd), jnp.float32)
    sum_zero = jnp.zeros((local_heads, feat_width), jnp.float32)
    local_state = jnp.sum(block_states, axis=0)
    local_sum = jnp.sum(block_sums, axis=0)
    earlier_state, earlier_sum = prefix(
        (local_state, local_sum), "ctx", add_pair, (state_zero, sum_zero)
    )
    inner_state = jnp.concatenate([state_zero[None], jnp.cumsum(block_states, axis=0)[:-1]], axis=0)
    inner_sum = jnp.concatenate([sum_zero[None], jnp.cumsum(block_sums, axis=0)[:-1]], axis=0)
    prefix_state = (earlier_state[None] + inner_state).astype(jnp.bfloat16)
    prefix_sum = (earlier_sum[None] + inner_sum).astype(jnp.bfloat16)
    num_state = jnp.einsum("btkf,bkfd->btkd", qf, prefix_state, preferred_element_type=jnp.float32)
    den_state = jnp.einsum("btkf,bkf->btk", qf, prefix_sum, preferred_element_type=jnp.float32)
    qblk = normed_queries.reshape(nblocks, BLOCK, local_heads, size_hd)
    kblk = normed_keys.reshape(nblocks, BLOCK, local_heads, size_hd)
    scores = jnp.einsum("btkd,bpkd->bktp", qblk, kblk, preferred_element_type=jnp.float32)
    causal = (
        jnp.arange(BLOCK, dtype=jnp.int32)[:, None] >= jnp.arange(BLOCK, dtype=jnp.int32)[None, :]
    ).astype(jnp.float32)
    weights = (score_scale * scores / size_hd) ** 4 * causal[None, None]
    den_diag = jnp.sum(weights, axis=-1).transpose(0, 2, 1)
    weights_b = weights.astype(jnp.bfloat16)
    num_diag = jnp.einsum("bktp,bpkd->btkd", weights_b, vbk, preferred_element_type=jnp.float32)
    attended = (num_diag + num_state) / (1.0 + den_diag + den_state)[..., None]
    attended = attended.astype(jnp.bfloat16).reshape(length, local_heads * size_hd)
    partial_out = jnp.dot(attended, out_weight, preferred_element_type=jnp.float32)
    mixed = lax.psum_scatter(
        partial_out.astype(jnp.bfloat16), "head", scatter_dimension=1, tiled=True
    )
    return mixed


def solution(mesh):
    in_specs = (
        P("ctx", "head"),
        P(None, None, "head"),
        P("head", None),
        P("head", None, None),
        P("head", None, None),
    )
    out_specs = P("ctx", "head")
    return jax.shard_map(shards, mesh=mesh, in_specs=in_specs, out_specs=out_specs, check_vma=False)
```

profile of v0, /device:TPU:480, one launch (start us, length us, event | category | flops | bytes accessed | tf_op | source)
XLA Modules:
  0.0 702.0 jit_solution(11091749225744624335)
XLA Ops:
  7.3 4.7 copy.17
  12.3 139.4 %all-gather.4.cloned.1.call-done = bf16[256,4096]{1,0:T(8,128)(2,1)} async-done(((bf16[256,128]{1,0:T(8,128)(2,1)}), bf16[256,4096]{1,0:T(8,128)(2,1)}) %all-gather.4.cloned.1.call-update) | async-done | bytes 2097168 | tf_op jit(solution)/shard_map/all_gather | solution.py:83
  151.7 3.5 fusion.3
  156.1 1.7 convolution_convert_fusion.1
  158.6 27.5 %all_gather.13 = bf16[16,1,4096]{2,1,0:T(2,128)(2,1)} all-gather(bf16[1,1,4096]{2,1,0:T(2,128)(2,1)S(1)} %convert_element_type.187), channel_id=1, replica_groups=mesh['ctx'=16,'head'=32] {'ctx'}, dimensions={0}, use_global_device_ids=true | all-gather | bytes 139264 | tf_op jit(solution)/shard_map/all_gather | solution.py:17
  187.7 2.0 multiply_convert_fusion
  189.8 151.9 %all-gather.6.cloned.1.call-done = bf16[65536,128]{1,0:T(8,128)(2,1)} async-done(((bf16[4096,128]{1,0:T(8,128)(2,1)}), bf16[65536,128]{1,0:T(8,128)(2,1)}) %all-gather.6.cloned.1.call-update) | async-done | bytes 16777232 | tf_op jit(solution)/shard_map/all_gather | solution.py:17
  341.9 32.0 %while.12 = (s32[]{:T(128)}, f32[1,4096,128]{2,1,0:T(8,128)S(1)}, f32[1,4096]{1,0:T(1,128)S(1)}, s32[]{:T(128)}, bf16[16,1,4096,128]{3,2,1,0:T(8,128)(2,1)}, /*i...) while((s32[]{:T(128)}, f32[1,4096,128]{2,1,0:T(8,128)S(1)}, f32[1,4096]{1,0:T(1,128)S(1)}, ...), condition=%wide.region_4.0_spmd, body=%wide.region_3.0_spmd.sunk | while | flops 1056773 | bytes 5283975 | solution.py:31
  341.9 1.5 convert_add_fusion.4
  344.2 1.5 convert_add_fusion.4
  346.5 1.5 convert_add_fusion.4
  348.7 1.5 convert_add_fusion.4
  353.3 1.5 convert_add_fusion.4
  355.6 1.5 convert_add_fusion.4
  357.9 1.5 convert_add_fusion.4
  360.2 1.5 convert_add_fusion.4
  362.4 1.5 convert_add_fusion.4
  364.7 1.5 convert_add_fusion.4
  367.0 1.5 convert_add_fusion.4
  373.9 2.1 fusion.73
  377.2 1.9 convolution_convert_fusion
  379.1 2.5 copy.25
  381.6 312.3 %reduce-scatter.4.cloned.1.call-done = bf16[128,256]{1,0:T(8,128)(2,1)} async-done(((bf16[4096,256]{1,0:T(8,128)(2,1)}), bf16[128,256]{1,0:T(8,128)(2,1)}) %reduce-scatter.4.cloned.1.call-update) | async-done | bytes 65552
  693.9 1.6 copy.26
  (49 shorter events, 20.8 us)
Async XLA Ops:
  6.5 370.7 %copy-start = (bf16[128,4096]{1,0:T(8,128)(2,1)S(1)}, bf16[128,4096]{1,0:T(8,128)(2,1)}, u32[]{:S(2)}) copy-start(bf16[128,4096]{1,0:T(8,128)(2,1)} %param.9) | copy-start | bytes 3145732
  6.5 145.1 %all-gather.4.cloned.1.call-start = ((), (), s32[]{:S(2)}) async-start(), calls=%async_computation.1 | async-start | bytes 2162688 | tf_op jit(solution)/shard_map/all_gather | solution.py:83
  7.3 4.8 copy-start.3
  7.3 4.8 copy-start.4
  7.3 334.4 %all-gather.6.cloned.1.call-start = ((), (), s32[]{:S(2)}) async-start(), calls=%async_computation.2 | async-start | bytes 17825792 | tf_op jit(solution)/shard_map/all_gather | solution.py:17
  157.9 536.0 %reduce-scatter.4.cloned.1.call-start = ((), (), s32[]{:S(2)}) async-start(), calls=%async_computation.3 | async-start | bytes 2162688
  373.8 2.2 copy-start.1
  376.1 1.2 copy-start.2
Sparse Core Ops, SparseCore 0:
  11.4 140.2 all-gather.3
  158.0 183.6 all-gather.5
  381.7 312.0 reduce-scatter.3
where the time goes:
time: 712 us; the launch traced here: 702 us
  waiting for transfers between devices  604 us (85%)
  other arithmetic  35.1 us (5%)
  blocking collectives  27.5 us (4%)
  between operations  13.2 us (2%)
  matrix products  12.4 us (2%)
  local copies, waits for them, and re-layouts  9.08 us (1%)
    unnamed x4, waiting for transfers between devices  313 us
    all_gather x1, waiting for transfers between devices, prefix(): lax.all_gather(a.astype(kind), axis)  152 us
    all_gather x1, waiting for transfers between devices, shards(): lax.all_gather(tokens, 'head', axis=1, tiled=True)  139 us
    add x28, other arithmetic, add_pair(): return (earlier[0] + later[0], earlier[1] + later[1])  31.6 us
    all_gather x1, blocking collectives, prefix(): lax.all_gather(a.astype(kind), axis)  27.5 us
  transfers between devices with their start and end apart: 3, of which 3 were waited for; matrix products, arithmetic and copies ran while one was open for 1% of the time, Pallas kernels for 0%

commit v1 on v0

v1 whole, which is shorter than its diff:
```python
import math

import jax
import jax.numpy as jnp
from jax import lax
from jax.experimental import pallas as pl
from jax.experimental.pallas import tpu as pltpu
from jax.sharding import PartitionSpec as P

MESH = pl.DeviceIdType.MESH
BLOCK = 256
HALF = 128
QUARTER = 64
HD = 128
RING = 4
SHIFTS = (0, 3, 1, 2)

score_scale = 2.0


def hadamard_table(size_hd):
    row_index = jnp.arange(size_hd, dtype=jnp.int32)[:, None]
    col_index = jnp.arange(size_hd, dtype=jnp.int32)[None, :]
    common = jnp.bitwise_and(row_index, col_index)
    parity = jnp.zeros((size_hd, size_hd), jnp.int32)
    for bit_place in range(size_hd.bit_length() - 1):
        parity = parity + jnp.bitwise_and(jnp.right_shift(common, bit_place), 1)
    return 1.0 - 2.0 * jnp.bitwise_and(parity, 1).astype(jnp.float32)


def sketch_matrix(signs, rows):
    size_hd = signs.shape[-1]
    hadamard = hadamard_table(size_hd)
    selector = (jnp.arange(size_hd, dtype=jnp.int32)[:, None] == rows[..., None, :]).astype(
        jnp.float32
    )
    columns = jnp.einsum("de,kief->kidf", hadamard, selector, precision=lax.Precision.HIGHEST)
    signed = (2 * signs - 1).astype(jnp.float32)
    return (signed[..., None] * columns).astype(jnp.bfloat16)


def dot(left, right):
    return jnp.dot(left, right, preferred_element_type=jnp.float32)


def dot_t(left, right):
    return lax.dot_general(left, right, (((1,), (1,)), ((), ())), preferred_element_type=jnp.float32)


def turn(place, step):
    return lax.rem(place + step, RING)


def kernel(
    x_ref, w_ref, wo_ref, sk_ref, out_ref,
    xbuf, wv, wov, acc, vb, fb, qf, num, wsum,
    s1, r1, s2, r2, s3, r3, t1,
    load_sem, z_send, z_recv, ag_send, ag_recv,
    kv_send, kv_pass, kv_recv, rs1_send, rs1_recv, rs2_send, rs2_recv, rs3_send, rs3_recv,
):
    head = lax.axis_index("head")
    ctx = lax.axis_index("ctx")
    chips = lax.axis_size("ctx") // 2
    z = lax.div(head, RING * RING)
    y = lax.rem(lax.div(head, RING), RING)
    x = lax.rem(head, RING)
    zl = lax.div(ctx, 2)
    core = lax.rem(ctx, 2)
    other_core = ctx + 1 - 2 * core
    z_partner = (1 - z) * RING * RING + y * RING + x
    sent = []

    def remote(src, dst, send_sem, recv_sem, **device):
        return pltpu.make_async_remote_copy(
            src_ref=src, dst_ref=dst, send_sem=send_sem, recv_sem=recv_sem,
            device_id=device, device_id_type=MESH,
        )

    def head_at(zz, eta, a, b, first_is_y):
        if first_is_y:
            return zz * RING * RING + a * RING + b
        return zz * RING * RING + b * RING + a

    own_block = xbuf.at[:, pl.ds(pl.multiple_of(head * HD, HD), HD)]
    load_x = pltpu.make_async_copy(x_ref, own_block, load_sem.at[0])
    load_w = pltpu.make_async_copy(w_ref, wv, load_sem.at[1])
    load_wo = pltpu.make_async_copy(wo_ref, wov, load_sem.at[2])
    load_x.start()
    load_w.start()
    load_wo.start()
    barrier = pltpu.get_barrier_semaphore()
    for step in (1, 2, 3):
        for place in (z * 16 + y * RING + turn(x, step), z * 16 + turn(y, step) * RING + x):
            pl.semaphore_signal(barrier, inc=1, device_id={"head": place}, device_id_type=MESH)
    pl.semaphore_signal(barrier, inc=1, device_id={"head": z_partner}, device_id_type=MESH)
    pl.semaphore_signal(barrier, inc=1, device_id={"ctx": other_core}, device_id_type=MESH)

    @pl.when(zl > 0)
    def _():
        pl.semaphore_signal(barrier, inc=1, device_id={"ctx": ctx - 2}, device_id_type=MESH)

    @pl.when(zl < chips - 1)
    def _():
        pl.semaphore_signal(barrier, inc=1, device_id={"ctx": ctx + 2}, device_id_type=MESH)

    acc[...] = jnp.zeros_like(acc)
    pl.semaphore_wait(barrier, 8 + lax.min(zl, 1) + lax.min(chips - 1 - zl, 1))

    load_x.wait()

    z_copy = remote(own_block, own_block, z_send, z_recv, head=z_partner)
    z_copy.start()
    sent.append(z_copy)

    def line(stage, eta, phase, shift):
        first_is_y = eta == 1
        a, b = (y, x) if first_is_y else (x, y)
        zz = z if stage == 0 else 1 - z
        base = (stage * 2 + eta) * 20 + (0 if phase == 0 else 4 + 4 * shift)
        pos = a if phase == 0 else b

        def device(place):
            return head_at(z, eta, place, b, first_is_y) if phase == 0 else head_at(z, eta, a, place, first_is_y)

        def piece(place, low, count):
            if phase == 0:
                t = head_at(zz, eta, place, b, first_is_y)
            else:
                t = head_at(zz, eta, turn(a, SHIFTS[shift]), place, first_is_y)
            return xbuf.at[pl.ds(eta * HALF + low, count), pl.ds(pl.multiple_of(t * HD, HD), HD)]

        def copy(k, what, step):
            return remote(what, what, ag_send.at[base + k], ag_recv.at[base + k], head=device(turn(pos, step)))

        def send(k, what, step):
            one = copy(k, what, step)
            one.start()
            sent.append(one)

        def start():
            send(0, piece(pos, 0, HALF), 1)
            send(1, piece(pos, 0, HALF), 3)

        def relay(side):
            if side == 0:
                copy(0, piece(turn(pos, 3), 0, HALF), 1).wait_recv()
                send(2, piece(turn(pos, 3), 0, QUARTER), 1)
            else:
                copy(1, piece(turn(pos, 1), 0, HALF), 3).wait_recv()
                send(3, piece(turn(pos, 1), QUARTER, QUARTER), 3)

        def finish():
            copy(2, piece(turn(pos, 2), 0, QUARTER), 1).wait_recv()
            copy(3, piece(turn(pos, 2), QUARTER, QUARTER), 3).wait_recv()

        return start, relay, finish

    def spread(stage, filler):
        first = [line(stage, eta, 0, 0) for eta in (0, 1)]
        second = [[line(stage, eta, 1, shift) for shift in range(4)] for eta in (0, 1)]
        for eta in (0, 1):
            first[eta][0]()
        for eta in (0, 1):
            second[eta][0][0]()
        filler()
        for side in (0, 1):
            for eta in (0, 1):
                first[eta][1](side)
                second[eta][1 + side][0]()
        for eta in (0, 1):
            for side in (0, 1):
                second[eta][0][1](side)
        for eta in (0, 1):
            first[eta][2]()
            second[eta][3][0]()
        for shift in (1, 2, 3):
            for side in (0, 1):
                for eta in (0, 1):
                    second[eta][shift][1](side)
        for shift in range(4):
            for eta in (0, 1):
                second[eta][shift][2]()

    chunk = 4 * HD

    def project(zz):
        def one(k, carry):
            low = pl.multiple_of(zz * (16 * HD) + k * chunk, chunk)
            acc[...] += dot(xbuf[:, pl.ds(low, chunk)], wv[pl.ds(low, chunk), :])
            return carry

        lax.fori_loop(0, 4, one, 0)

    spread(0, lambda: None)
    load_w.wait()
    z_block = xbuf.at[:, pl.ds(pl.multiple_of(z_partner * HD, HD), HD)]
    remote(z_block, z_block, z_send, z_recv, head=z_partner).wait_recv()
    spread(1, lambda: project(z))
    project(1 - z)

    def normalize(raw):
        return (raw * lax.rsqrt(jnp.mean(raw * raw, axis=-1, keepdims=True) + 1e-06)).astype(jnp.bfloat16)

    factor = score_scale * score_scale / (HD * math.sqrt(QUARTER))

    def twice(normed):
        return factor * dot(normed, sk_ref[0]) * dot(normed, sk_ref[1])

    kn = normalize(acc[:, HD : 2 * HD])
    kf = twice(kn)
    low_half = lax.broadcasted_iota(jnp.int32, (HALF, HD), 1) < QUARTER
    fb[ctx] = jnp.where(low_half, kf[:HALF], kf[HALF:]).astype(jnp.bfloat16)
    vb[ctx] = acc[:, 2 * HD :].astype(jnp.bfloat16)
    qn = normalize(acc[:, :HD])
    qd = twice(qn)
    lanes_low = lax.broadcasted_iota(jnp.int32, (BLOCK, HD), 1) < QUARTER
    qf[0] = jnp.where(lanes_low, qd, 0.0).astype(jnp.bfloat16)
    qf[1] = jnp.where(lanes_low, 0.0, qd).astype(jnp.bfloat16)

    def kv(slot, sems, offset, target):
        return (
            remote(vb.at[slot], vb.at[slot], sems.at[2 * slot], kv_recv.at[2 * slot], ctx=target),
            remote(fb.at[slot], fb.at[slot], sems.at[2 * slot + 1], kv_recv.at[2 * slot + 1], ctx=target),
        )

    def up(slot):
        return kv(slot, kv_send, 0, ctx + 2)

    def over(slot):
        return kv(slot, kv_pass, 0, other_core)

    def arrive(slot):
        for one in kv(slot, kv_pass, 0, other_core):
            one.wait_recv()

    @pl.when(zl < chips - 1)
    def _():
        for one in up(ctx):
            one.start()

    @pl.when(core == 0)
    def _():
        for one in over(ctx):
            one.start()

    scores = dot_t(qn, kn)
    causal = (
        lax.broadcasted_iota(jnp.int32, (BLOCK, BLOCK), 0)
        >= lax.broadcasted_iota(jnp.int32, (BLOCK, BLOCK), 1)
    )
    scaled = scores * (score_scale / HD)
    square = scaled * scaled
    weights = jnp.where(causal, square * square, 0.0)
    wsum[...] = weights[:, :HD] + weights[:, HD:]
    num[...] = dot(weights.astype(jnp.bfloat16), vb[ctx])

    def attend(slot):
        packed = fb[slot]
        left = dot_t(qf[0], packed)
        right = dot_t(qf[1], packed)
        left = left * left
        right = right * right
        wsum[...] += left + right
        both = jnp.concatenate([left.astype(jnp.bfloat16), right.astype(jnp.bfloat16)], axis=1)
        num[...] += dot(both, vb[slot])

    @pl.when(core == 1)
    def _():
        arrive(2 * zl)
        attend(2 * zl)

    def earlier(s, carry):
        chip = zl - 1 - s
        slot = 2 * chip + core
        arrive(slot)

        @pl.when(zl < chips - 1)
        def _():
            for one in up(slot):
                one.start()

        for one in over(slot):
            one.start()
        attend(slot)
        second = 2 * chip + 1 - core
        arrive(second)
        attend(second)
        return carry

    lax.fori_loop(0, zl, earlier, 0)

    total = 1.0 + jnp.sum(wsum[...], axis=-1, keepdims=True)
    attended = (num[...] / total).astype(jnp.bfloat16)

    load_wo.wait()
    for stage in (0, 1):
        zz = 1 - z if stage == 0 else z
        for row in range(RING):
            low = pl.multiple_of((zz * 16 + row * RING) * HD, RING * HD)
            product = dot(attended, wov[:, pl.ds(low, RING * HD)]).astype(jnp.bfloat16)
            for col in range(RING):
                tile = product[:, col * HD : (col + 1) * HD]
                s1[0, stage, row, col] = tile[:HALF]
                s1[1, stage, col, row] = tile[HALF:]

    def rs1(stage, eta, step):
        a, b = (y, x) if eta == 0 else (x, y)
        k = (stage * 2 + eta) * 3 + step - 1
        to = turn(a, step)
        return remote(
            s1.at[eta, stage, to], r1.at[eta, stage, step - 1], rs1_send.at[k], rs1_recv.at[k],
            head=head_at(z, eta, to, b, eta == 0),
        )

    def rs2(stage, eta, step):
        a, b = (y, x) if eta == 0 else (x, y)
        k = (stage * 2 + eta) * 3 + step - 1
        to = turn(b, step)
        return remote(
            s2.at[eta, stage, to], r2.at[eta, stage, step - 1], rs2_send.at[k], rs2_recv.at[k],
            head=head_at(z, eta, a, to, eta == 0),
        )

    def rs3(eta):
        return remote(s3.at[eta], r3.at[eta], rs3_send.at[eta], rs3_recv.at[eta], head=z_partner)

    for stage in (0, 1):
        for step in (2, 1, 3):
            for eta in (0, 1):
                one = rs1(stage, eta, step)
                one.start()
                sent.append(one)

    f32 = jnp.float32

    def reduce_first(stage):
        for step in (1, 3, 2):
            for eta in (0, 1):
                rs1(stage, eta, step).wait_recv()
        for eta in (0, 1):
            a = y if eta == 0 else x
            for b in range(RING):
                value = s1[eta, stage, a, b].astype(f32)
                for k in range(3):
                    value = value + r1[eta, stage, k, b].astype(f32)
                s2[eta, stage, b] = value.astype(jnp.bfloat16)
        for step in (2, 1, 3):
            for eta in (0, 1):
                one = rs2(stage, eta, step)
                one.start()
                sent.append(one)

    def reduce_second(stage, eta):
        a, b = (y, x) if eta == 0 else (x, y)
        value = s1[eta, stage, a, b].astype(f32)
        for k in range(3):
            value = value + r1[eta, stage, k, b].astype(f32)
        for step in (1, 3, 2):
            rs2(stage, eta, step).wait_recv()
        for k in range(3):
            value = value + r2[eta, stage, k].astype(f32)
        return value

    reduce_first(0)
    for eta in (0, 1):
        s3[eta] = reduce_second(0, eta).astype(jnp.bfloat16)
    for eta in (0, 1):
        one = rs3(eta)
        one.start()
        sent.append(one)
    reduce_first(1)
    for eta in (0, 1):
        t1[eta] = reduce_second(1, eta)
    for eta in (0, 1):
        rs3(eta).wait_recv()
        out_ref[pl.ds(eta * HALF, HALF), :] = (t1[eta] + r3[eta].astype(f32)).astype(jnp.bfloat16)

    for one in sent:
        one.wait_send()

    @pl.when(zl < chips - 1)
    def _():
        for one in up(ctx):
            one.wait_send()

    @pl.when(core == 0)
    def _():
        for one in over(ctx):
            one.wait_send()

    def drain(s, carry):
        slot = 2 * (zl - 1 - s) + core

        @pl.when(zl < chips - 1)
        def _():
            for one in up(slot):
                one.wait_send()

        for one in over(slot):
            one.wait_send()
        return carry

    lax.fori_loop(0, zl, drain, 0)


def shards(tokens, qkv_weight, out_weight, signs, rows):
    width = qkv_weight.shape[0]
    parts = lax.axis_size("ctx")
    flat_weight = qkv_weight.reshape(width, 3 * HD)
    sketch = sketch_matrix(signs, rows)[0]
    sketch = jnp.concatenate([sketch, sketch], axis=-1)
    bf16, f32 = jnp.bfloat16, jnp.float32
    anywhere = pl.BlockSpec(memory_space=pl.ANY)
    vmem = pl.BlockSpec(memory_space=pltpu.VMEM)
    dma = pltpu.SemaphoreType.DMA
    return pl.pallas_call(
        kernel,
        out_shape=jax.ShapeDtypeStruct((BLOCK, HD), bf16),
        in_specs=[anywhere, anywhere, anywhere, vmem],
        out_specs=vmem,
        scratch_shapes=[
            pltpu.VMEM((BLOCK, width), bf16),
            pltpu.VMEM((width, 3 * HD), bf16),
            pltpu.VMEM((HD, width), bf16),
            pltpu.VMEM((BLOCK, 3 * HD), f32),
            pltpu.VMEM((parts, BLOCK, HD), bf16),
            pltpu.VMEM((parts, HALF, HD), bf16),
            pltpu.VMEM((2, BLOCK, HD), bf16),
            pltpu.VMEM((BLOCK, HD), f32),
            pltpu.VMEM((BLOCK, HD), f32),
            pltpu.VMEM((2, 2, RING, RING, HALF, HD), bf16),
            pltpu.VMEM((2, 2, 3, RING, HALF, HD), bf16),
            pltpu.VMEM((2, 2, RING, HALF, HD), bf16),
            pltpu.VMEM((2, 2, 3, HALF, HD), bf16),
            pltpu.VMEM((2, HALF, HD), bf16),
            pltpu.VMEM((2, HALF, HD), bf16),
            pltpu.VMEM((2, HALF, HD), f32),
            dma((3,)),
            dma,
            dma,
            dma((80,)),
            dma((80,)),
            dma((2 * parts,)),
            dma((2 * parts,)),
            dma((2 * parts,)),
            dma((12,)),
            dma((12,)),
            dma((12,)),
            dma((12,)),
            dma((2,)),
            dma((2,)),
        ],
        compiler_params=pltpu.CompilerParams(collective_id=0, has_side_effects=True),
    )(tokens, flat_weight, out_weight, sketch)


def solution(mesh):
    in_specs = (
        P("ctx", "head"),
        P(None, None, "head"),
        P("head", None),
        P("head", None, None),
        P("head", None, None),
    )
    out_specs = P("ctx", "head")
    return jax.shard_map(shards, mesh=mesh, in_specs=in_specs, out_specs=out_specs, check_vma=False)
```

time: 712 us -> 104 us (0.15); the launches traced: 702 us -> 104 us
  waiting for transfers between devices: 604 us -> 0 us
  Pallas kernels: 0 us -> 95.5 us
  other arithmetic: 35.1 us -> 0.73 us
  blocking collectives: 27.5 us -> 0 us
  between operations: 13.2 us -> 0.04 us
  matrix products: 12.4 us -> 0.34 us
    unnamed x4 -> x0, waiting for transfers between devices: 313 us -> none
    all_gather x2 -> x0, waiting for transfers between devices: 291 us -> none  [the longest x1 152 us: prefix(): lax.all_gather(a.astype(kind), axis)]
    pallas_call x0 -> x1, Pallas kernels: none -> 95.5 us  [shards(): pl.pallas_call(kernel, out_shape=jax.ShapeDtypeStruct((BLOCK, HD), bf16),...]
    add x29 -> x0, other arithmetic: 31.7 us -> none  [the longest x28 31.6 us: add_pair(): return (earlier[0] + later[0], earlier[1] + later[1])]
    all_gather x1 -> x0, blocking collectives: 27.5 us -> none  [prefix(): lax.all_gather(a.astype(kind), axis)]
    dot_general x8 -> x0, matrix products: 12.1 us -> none  [the longest x1 3.53 us: shards(): jnp.dot(lax.all_gather(tokens, 'head', axis=1, tiled=True), flat_weight,...]
  transfers between devices with their start and end apart: 3 -> 0, of which waited for: 3 -> 0; matrix products, arithmetic and copies ran while one was open for 1% -> 0% of each run, Pallas kernels for 0% -> 0%
where the time goes in v1:
time: 104 us
  Pallas kernels  95.5 us (92%)
  local copies, waits for them, and re-layouts  7.48 us (7%)
    pallas_call x1, Pallas kernels, shards(): pl.pallas_call(kernel, out_shape=jax.ShapeDtypeStruct((BLOCK, HD), bf16),...  95.5 us
    unnamed x6, local copies, waits for them, and re-layouts  4.68 us
    reshape x1, local copies, waits for them, and re-layouts, shards(): flat_weight = qkv_weight.reshape(width, 3 * HD)  2.8 us

profile of v1, /device:TPU:480, one launch (start us, length us, event | category | flops | bytes accessed | tf_op | source)
XLA Modules:
  0.0 104.1 jit_solution(16874972263965548665)
XLA Ops:
  0.0 3.2 %copy.8 = bf16[4096,3,128]{0,2,1:T(8,128)(2,1)S(1)} copy(bf16[4096,3,128]{2,0,1:T(8,128)(2,1)} %param.6) | data formatting | bytes 6291456 | tf_op args[1]
  3.2 0.0 copy-start
  3.2 0.0 copy-start.1
  3.2 2.8 %copy.10.w_ref = bf16[4096,384]{1,0:T(8,128)(2,1)} copy(bf16[4096,384]{0,1:T(8,128)(2,1)S(1)} %bitcast.19) | data formatting | bytes 6291456 | tf_op jit(solution)/shard_map/reshape | solution.py:409
  6.0 0.0 copy-done
  6.0 0.0 copy-done.1
  6.0 0.3 fusion.2
  6.4 0.7 pad_maximum_fusion.sk_ref
  7.1 95.5 %shard_map.55 = bf16[256,128]{1,0:T(8,128)(2,1)} custom-call(bf16[256,128]{1,0:T(8,128)(2,1)} %x_ref.1, bf16[4096,384]{1,0:T(8,128)(2,1)} %copy.10.w_ref, bf16[128,4096]{1,0:T(8,128)(2,1)} %wo_ref.1, bf16[2,128,128]{2,1,0:T(8,128)(2,1)} %pad_maximum_fusion.sk_ref), custom_call_target="tpu_custom_call" | custom-call | tf_op jit(solution)/shard_map/pallas_call | solution.py:416
  102.6 1.5 %copy.13 = bf16[256,128]{1,0:T(8,128)(2,1)} copy(bf16[256,128]{1,0:T(8,128)(2,1)} %shard_map.55) | data formatting | bytes 131072
  (1 shorter events, 0.0 us)
Async XLA Ops:
  3.2 2.8 %copy-start = (s32[1,2,128]{2,1,0:T(2,128)S(1)}, s32[1,2,128]{2,1,0:T(2,128)}, u32[]{:S(2)}) copy-start(s32[1,2,128]{2,1,0:T(2,128)} %param.8) | copy-start | bytes 3076
  3.2 2.8 %copy-start.1 = (s32[1,2,64]{2,1,0:T(2,128)S(1)}, s32[1,2,64]{2,1,0:T(2,128)}, u32[]{:S(2)}) copy-start(s32[1,2,64]{2,1,0:T(2,128)} %param.9) | copy-start | bytes 1540

commit v2 on v1

--- a/solution.py
+++ b/solution.py
@@ -18,27 +18,6 @@
 score_scale = 2.0
 
 
-def hadamard_table(size_hd):
-    row_index = jnp.arange(size_hd, dtype=jnp.int32)[:, None]
-    col_index = jnp.arange(size_hd, dtype=jnp.int32)[None, :]
-    common = jnp.bitwise_and(row_index, col_index)
-    parity = jnp.zeros((size_hd, size_hd), jnp.int32)
-    for bit_place in range(size_hd.bit_length() - 1):
-        parity = parity + jnp.bitwise_and(jnp.right_shift(common, bit_place), 1)
-    return 1.0 - 2.0 * jnp.bitwise_and(parity, 1).astype(jnp.float32)
-
-
-def sketch_matrix(signs, rows):
-    size_hd = signs.shape[-1]
-    hadamard = hadamard_table(size_hd)
-    selector = (jnp.arange(size_hd, dtype=jnp.int32)[:, None] == rows[..., None, :]).astype(
-        jnp.float32
-    )
-    columns = jnp.einsum("de,kief->kidf", hadamard, selector, precision=lax.Precision.HIGHEST)
-    signed = (2 * signs - 1).astype(jnp.float32)
-    return (signed[..., None] * columns).astype(jnp.bfloat16)
-
-
 def dot(left, right):
     return jnp.dot(left, right, preferred_element_type=jnp.float32)
 
@@ -52,11 +31,11 @@
 
 
 def kernel(
-    x_ref, w_ref, wo_ref, sk_ref, out_ref,
-    xbuf, wv, wov, acc, vb, fb, qf, num, wsum,
-    s1, r1, s2, r2, s3, r3, t1,
+    x_ref, w_ref, wo_ref, signs_ref, rows_ref, out_ref,
+    xbuf, wv, wov, acc, kvb, sk, qf, num, wsum,
+    s1, ra, r1, s2, r2, s3, r3, t1,
     load_sem, z_send, z_recv, ag_send, ag_recv,
-    kv_send, kv_pass, kv_recv, rs1_send, rs1_recv, rs2_send, rs2_recv, rs3_send, rs3_recv,
+    kv_send, kv_pass, kv_recv, rsa_send, rsa_recv, rs1_send, rs1_recv, rs2_send, rs2_recv, rs3_send, rs3_recv,
 ):
     head = lax.axis_index("head")
     ctx = lax.axis_index("ctx")
@@ -83,10 +62,14 @@
 
     own_block = xbuf.at[:, pl.ds(pl.multiple_of(head * HD, HD), HD)]
     load_x = pltpu.make_async_copy(x_ref, own_block, load_sem.at[0])
-    load_w = pltpu.make_async_copy(w_ref, wv, load_sem.at[1])
-    load_wo = pltpu.make_async_copy(wo_ref, wov, load_sem.at[2])
+    load_w = [
+        pltpu.make_async_copy(w_ref.at[j], wv.at[:, pl.ds(j * HD, HD)], load_sem.at[2 + j])
+        for j in range(3)
+    ]
+    load_wo = pltpu.make_async_copy(wo_ref, wov, load_sem.at[1])
     load_x.start()
-    load_w.start()
+    for one in load_w:
+        one.start()
     load_wo.start()
     barrier = pltpu.get_barrier_semaphore()
     for step in (1, 2, 3):
@@ -104,6 +87,17 @@
         pl.semaphore_signal(barrier, inc=1, device_id={"ctx": ctx + 2}, device_id_type=MESH)
 
     acc[...] = jnp.zeros_like(acc)
+
+    signed = (2 * signs_ref[0] - 1).astype(jnp.float32)
+    sampled = jnp.concatenate([rows_ref[0], rows_ref[0]], axis=1)
+    entry = lax.broadcasted_iota(jnp.int32, (HD, HD), 0)
+    for i in (0, 1):
+        common = jnp.bitwise_and(entry, sampled[i : i + 1, :])
+        for shift in (4, 2, 1):
+            common = jnp.bitwise_xor(common, jnp.right_shift(common, shift))
+        parity = jnp.bitwise_and(common, 1)
+        sk[i] = (1 - 2 * parity).astype(jnp.float32).astype(jnp.bfloat16)
+
     pl.semaphore_wait(barrier, 8 + lax.min(zl, 1) + lax.min(chips - 1 - zl, 1))
 
     load_x.wait()
@@ -192,7 +186,8 @@
         lax.fori_loop(0, 4, one, 0)
 
     spread(0, lambda: None)
-    load_w.wait()
+    for one in load_w:
+        one.wait()
     z_block = xbuf.at[:, pl.ds(pl.multiple_of(z_partner * HD, HD), HD)]
     remote(z_block, z_block, z_send, z_recv, head=z_partner).wait_recv()
     spread(1, lambda: project(z))
@@ -204,34 +199,35 @@
     factor = score_scale * score_scale / (HD * math.sqrt(QUARTER))
 
     def twice(normed):
-        return factor * dot(normed, sk_ref[0]) * dot(normed, sk_ref[1])
+        wide = normed.astype(jnp.float32)
+        first = dot((wide * signed[0:1, :]).astype(jnp.bfloat16), sk[0])
+        second = dot((wide * signed[1:2, :]).astype(jnp.bfloat16), sk[1])
+        return factor * first * second
 
     kn = normalize(acc[:, HD : 2 * HD])
     kf = twice(kn)
     low_half = lax.broadcasted_iota(jnp.int32, (HALF, HD), 1) < QUARTER
-    fb[ctx] = jnp.where(low_half, kf[:HALF], kf[HALF:]).astype(jnp.bfloat16)
-    vb[ctx] = acc[:, 2 * HD :].astype(jnp.bfloat16)
+    kvb[ctx, 0] = jnp.where(low_half, kf[:HALF], kf[HALF:]).astype(jnp.bfloat16)
+    kvb[ctx, 1] = acc[:HALF, 2 * HD :].astype(jnp.bfloat16)
+    kvb[ctx, 2] = acc[HALF:, 2 * HD :].astype(jnp.bfloat16)
     qn = normalize(acc[:, :HD])
     qd = twice(qn)
     lanes_low = lax.broadcasted_iota(jnp.int32, (BLOCK, HD), 1) < QUARTER
     qf[0] = jnp.where(lanes_low, qd, 0.0).astype(jnp.bfloat16)
     qf[1] = jnp.where(lanes_low, 0.0, qd).astype(jnp.bfloat16)
 
-    def kv(slot, sems, offset, target):
-        return (
-            remote(vb.at[slot], vb.at[slot], sems.at[2 * slot], kv_recv.at[2 * slot], ctx=target),
-            remote(fb.at[slot], fb.at[slot], sems.at[2 * slot + 1], kv_recv.at[2 * slot + 1], ctx=target),
-        )
+    def kv(slot, piece, sems, target):
+        k = 3 * slot + piece
+        return remote(kvb.at[slot, piece], kvb.at[slot, piece], sems.at[k], kv_recv.at[k], ctx=target)
 
     def up(slot):
-        return kv(slot, kv_send, 0, ctx + 2)
+        return [kv(slot, piece, kv_send, ctx + 2) for piece in range(3)]
 
     def over(slot):
-        return kv(slot, kv_pass, 0, other_core)
-
-    def arrive(slot):
-        for one in kv(slot, kv_pass, 0, other_core):
-            one.wait_recv()
+        return [kv(slot, piece, kv_pass, other_core) for piece in range(3)]
+
+    def values(slot):
+        return kvb[slot, pl.ds(1, 2)].reshape(BLOCK, HD)
 
     @pl.when(zl < chips - 1)
     def _():
@@ -252,38 +248,40 @@
     square = scaled * scaled
     weights = jnp.where(causal, square * square, 0.0)
     wsum[...] = weights[:, :HD] + weights[:, HD:]
-    num[...] = dot(weights.astype(jnp.bfloat16), vb[ctx])
+    num[...] = dot(weights.astype(jnp.bfloat16), values(ctx))
 
     def attend(slot):
-        packed = fb[slot]
+        packed = kvb[slot, 0]
         left = dot_t(qf[0], packed)
         right = dot_t(qf[1], packed)
         left = left * left
         right = right * right
         wsum[...] += left + right
         both = jnp.concatenate([left.astype(jnp.bfloat16), right.astype(jnp.bfloat16)], axis=1)
-        num[...] += dot(both, vb[slot])
+        num[...] += dot(both, values(slot))
 
     @pl.when(core == 1)
     def _():
-        arrive(2 * zl)
+        for one in over(2 * zl):
+            one.wait_recv()
         attend(2 * zl)
 
     def earlier(s, carry):
         chip = zl - 1 - s
         slot = 2 * chip + core
-        arrive(slot)
-
-        @pl.when(zl < chips - 1)
-        def _():
-            for one in up(slot):
-                one.start()
-
-        for one in over(slot):
-            one.start()
+        for piece in range(3):
+            kv(slot, piece, kv_send, other_core).wait_recv()
+
+            @pl.when(zl < chips - 1)
+            def _():
+                kv(slot, piece, kv_send, ctx + 2).start()
+
+            kv(slot, piece, kv_pass, other_core).start()
+
         attend(slot)
         second = 2 * chip + 1 - core
-        arrive(second)
+        for one in over(second):
+            one.wait_recv()
         attend(second)
         return carry
 
@@ -303,13 +301,28 @@
                 s1[0, stage, row, col] = tile[:HALF]
                 s1[1, stage, col, row] = tile[HALF:]
 
-    def rs1(stage, eta, step):
+    PAIR = RING // 2
+
+    def ring(eta, step):
         a, b = (y, x) if eta == 0 else (x, y)
-        k = (stage * 2 + eta) * 3 + step - 1
         to = turn(a, step)
+        return to, head_at(z, eta, to, b, eta == 0)
+
+    def rsa(stage, eta, side):
+        k = (stage * 2 + eta) * 2 + side
+        far, _ = ring(eta, 2)
+        _, device = ring(eta, 1 if side == 0 else 3)
         return remote(
-            s1.at[eta, stage, to], r1.at[eta, stage, step - 1], rs1_send.at[k], rs1_recv.at[k],
-            head=head_at(z, eta, to, b, eta == 0),
+            s1.at[eta, stage, far, pl.ds(side * PAIR, PAIR)], ra.at[eta, stage, side],
+            rsa_send.at[k], rsa_recv.at[k], head=device,
+        )
+
+    def rs1(stage, eta, side, half):
+        k = ((stage * 2 + eta) * 2 + side) * 2 + half
+        to, device = ring(eta, 1 if side == 0 else 3)
+        return remote(
+            s1.at[eta, stage, to, pl.ds(half * PAIR, PAIR)], r1.at[eta, stage, side, pl.ds(half * PAIR, PAIR)],
+            rs1_send.at[k], rs1_recv.at[k], head=device,
         )
 
     def rs2(stage, eta, step):
@@ -324,24 +337,40 @@
     def rs3(eta):
         return remote(s3.at[eta], r3.at[eta], rs3_send.at[eta], rs3_recv.at[eta], head=z_partner)
 
+    def begin(one):
+        one.start()
+        sent.append(one)
+
+    ways = [(eta, side) for eta in (0, 1) for side in (0, 1)]
     for stage in (0, 1):
-        for step in (2, 1, 3):
-            for eta in (0, 1):
-                one = rs1(stage, eta, step)
-                one.start()
-                sent.append(one)
+        for eta, side in ways:
+            begin(rsa(stage, eta, side))
+        for eta, side in ways:
+            begin(rs1(stage, eta, side, 1 - side))
 
     f32 = jnp.float32
 
+    def relay_first(stage):
+        for eta, side in ways:
+            rsa(stage, eta, side).wait_recv()
+            to, _ = ring(eta, 1 if side == 0 else 3)
+            part = pl.ds(side * PAIR, PAIR)
+            s1[eta, stage, to, part] = (
+                s1[eta, stage, to, part].astype(f32) + ra[eta, stage, side].astype(f32)
+            ).astype(jnp.bfloat16)
+        for eta, side in ways:
+            begin(rs1(stage, eta, side, side))
+
     def reduce_first(stage):
-        for step in (1, 3, 2):
-            for eta in (0, 1):
-                rs1(stage, eta, step).wait_recv()
+        for eta, side in ways:
+            rs1(stage, eta, side, 1 - side).wait_recv()
+        for eta, side in ways:
+            rs1(stage, eta, side, side).wait_recv()
         for eta in (0, 1):
             a = y if eta == 0 else x
             for b in range(RING):
                 value = s1[eta, stage, a, b].astype(f32)
-                for k in range(3):
+                for k in range(2):
                     value = value + r1[eta, stage, k, b].astype(f32)
                 s2[eta, stage, b] = value.astype(jnp.bfloat16)
         for step in (2, 1, 3):
@@ -353,7 +382,7 @@
     def reduce_second(stage, eta):
         a, b = (y, x) if eta == 0 else (x, y)
         value = s1[eta, stage, a, b].astype(f32)
-        for k in range(3):
+        for k in range(2):
             value = value + r1[eta, stage, k, b].astype(f32)
         for step in (1, 3, 2):
             rs2(stage, eta, step).wait_recv()
@@ -361,6 +390,8 @@
             value = value + r2[eta, stage, k].astype(f32)
         return value
 
+    relay_first(0)
+    relay_first(1)
     reduce_first(0)
     for eta in (0, 1):
         s3[eta] = reduce_second(0, eta).astype(jnp.bfloat16)
@@ -406,9 +437,7 @@
 def shards(tokens, qkv_weight, out_weight, signs, rows):
     width = qkv_weight.shape[0]
     parts = lax.axis_size("ctx")
-    flat_weight = qkv_weight.reshape(width, 3 * HD)
-    sketch = sketch_matrix(signs, rows)[0]
-    sketch = jnp.concatenate([sketch, sketch], axis=-1)
+    by_kind = qkv_weight.transpose(1, 0, 2)
     bf16, f32 = jnp.bfloat16, jnp.float32
     anywhere = pl.BlockSpec(memory_space=pl.ANY)
     vmem = pl.BlockSpec(memory_space=pltpu.VMEM)
@@ -416,42 +445,45 @@
     return pl.pallas_call(
         kernel,
         out_shape=jax.ShapeDtypeStruct((BLOCK, HD), bf16),
-        in_specs=[anywhere, anywhere, anywhere, vmem],
+        in_specs=[anywhere, anywhere, anywhere, vmem, vmem],
         out_specs=vmem,
         scratch_shapes=[
             pltpu.VMEM((BLOCK, width), bf16),
             pltpu.VMEM((width, 3 * HD), bf16),
             pltpu.VMEM((HD, width), bf16),
             pltpu.VMEM((BLOCK, 3 * HD), f32),
-            pltpu.VMEM((parts, BLOCK, HD), bf16),
-            pltpu.VMEM((parts, HALF, HD), bf16),
+            pltpu.VMEM((parts, 3, HALF, HD), bf16),
+            pltpu.VMEM((2, HD, HD), bf16),
             pltpu.VMEM((2, BLOCK, HD), bf16),
             pltpu.VMEM((BLOCK, HD), f32),
             pltpu.VMEM((BLOCK, HD), f32),
             pltpu.VMEM((2, 2, RING, RING, HALF, HD), bf16),
-            pltpu.VMEM((2, 2, 3, RING, HALF, HD), bf16),
+            pltpu.VMEM((2, 2, 2, RING // 2, HALF, HD), bf16),
+            pltpu.VMEM((2, 2, 2, RING, HALF, HD), bf16),
             pltpu.VMEM((2, 2, RING, HALF, HD), bf16),
             pltpu.VMEM((2, 2, 3, HALF, HD), bf16),
             pltpu.VMEM((2, HALF, HD), bf16),
             pltpu.VMEM((2, HALF, HD), bf16),
             pltpu.VMEM((2, HALF, HD), f32),
-            dma((3,)),
+            dma((5,)),
             dma,
             dma,
             dma((80,)),
             dma((80,)),
-            dma((2 * parts,)),
-            dma((2 * parts,)),
-            dma((2 * parts,)),
-            dma((12,)),
-            dma((12,)),
+            dma((3 * parts,)),
+            dma((3 * parts,)),
+            dma((3 * parts,)),
+            dma((8,)),
+            dma((8,)),
+            dma((16,)),
+            dma((16,)),
             dma((12,)),
             dma((12,)),
             dma((2,)),
             dma((2,)),
         ],
         compiler_params=pltpu.CompilerParams(collective_id=0, has_side_effects=True),
-    )(tokens, flat_weight, out_weight, sketch)
+    )(tokens, by_kind, out_weight, signs, rows)
 
 
 def solution(mesh):

time: 104 us -> 92.2 us (0.89)
  local copies, waits for them, and re-layouts: 7.48 us -> 1.47 us
  Pallas kernels: 95.5 us -> 90.5 us
    pallas_call x1, Pallas kernels: 95.5 us -> 90.5 us  [shards(): pl.pallas_call(kernel, out_shape=jax.ShapeDtypeStruct((BLOCK, HD), bf16),...]
    unnamed x6 -> x1, local copies, waits for them, and re-layouts: 4.68 us -> 1.47 us
    reshape x1 -> x0, local copies, waits for them, and re-layouts: 2.8 us -> none  [shards(): flat_weight = qkv_weight.reshape(width, 3 * HD)]
where the time goes in v2:
time: 92.2 us; the launch traced here: 92 us
  Pallas kernels  90.5 us (98%)
  local copies, waits for them, and re-layouts  1.47 us (2%)
    pallas_call x1, Pallas kernels, shards(): pl.pallas_call(kernel, out_shape=jax.ShapeDtypeStruct((BLOCK, HD), bf16),...  90.5 us

profile of v2, /device:TPU:480, one launch (start us, length us, event | category | flops | bytes accessed | tf_op | source)
XLA Modules:
  0.0 92.0 jit_solution(17200890034475404646)
XLA Ops:
  0.0 90.5 %shard_map.55 = bf16[256,128]{1,0:T(8,128)(2,1)} custom-call(bf16[256,128]{1,0:T(8,128)(2,1)} %x_ref.1, bf16[3,4096,128]{2,1,0:T(8,128)(2,1)} %bitcast.1, bf16[128,4096]{1,0:T(8,128)(2,1)} %wo_ref.1, s32[1,2,128]{2,1,0:T(2,128)} %signs_ref.1, s32[1,2,64]{2,1,0:T(2,128)} %rows_ref.1), custom_call_target="tpu_custom_call" | custom-call | tf_op jit(solution)/shard_map/pallas_call | solution.py:445
  90.5 1.5 %copy.7 = bf16[256,128]{1,0:T(8,128)(2,1)} copy(bf16[256,128]{1,0:T(8,128)(2,1)} %shard_map.55) | data formatting | bytes 131072

commit v3 on v2

--- a/solution.py
+++ b/solution.py
@@ -60,7 +60,7 @@
             return zz * RING * RING + a * RING + b
         return zz * RING * RING + b * RING + a
 
-    own_block = xbuf.at[:, pl.ds(pl.multiple_of(head * HD, HD), HD)]
+    own_block = xbuf.at[head]
     load_x = pltpu.make_async_copy(x_ref, own_block, load_sem.at[0])
     load_w = [
         pltpu.make_async_copy(w_ref.at[j], wv.at[:, pl.ds(j * HD, HD)], load_sem.at[2 + j])
@@ -121,7 +121,7 @@
                 t = head_at(zz, eta, place, b, first_is_y)
             else:
                 t = head_at(zz, eta, turn(a, SHIFTS[shift]), place, first_is_y)
-            return xbuf.at[pl.ds(eta * HALF + low, count), pl.ds(pl.multiple_of(t * HD, HD), HD)]
+            return xbuf.at[t, eta, pl.ds(low, count)]
 
         def copy(k, what, step):
             return remote(what, what, ag_send.at[base + k], ag_recv.at[base + k], head=device(turn(pos, step)))
@@ -149,49 +149,58 @@
 
         return start, relay, finish
 
-    def spread(stage, filler):
+    def spread(stage, fillers):
         first = [line(stage, eta, 0, 0) for eta in (0, 1)]
         second = [[line(stage, eta, 1, shift) for shift in range(4)] for eta in (0, 1)]
         for eta in (0, 1):
             first[eta][0]()
         for eta in (0, 1):
             second[eta][0][0]()
-        filler()
+        fillers[0]()
         for side in (0, 1):
             for eta in (0, 1):
                 first[eta][1](side)
                 second[eta][1 + side][0]()
+        fillers[1]()
         for eta in (0, 1):
             for side in (0, 1):
                 second[eta][0][1](side)
+        fillers[2]()
         for eta in (0, 1):
             first[eta][2]()
             second[eta][3][0]()
+        fillers[3]()
         for shift in (1, 2, 3):
             for side in (0, 1):
                 for eta in (0, 1):
                     second[eta][shift][1](side)
-        for shift in range(4):
-            for eta in (0, 1):
-                second[eta][shift][2]()
-
-    chunk = 4 * HD
-
-    def project(zz):
-        def one(k, carry):
-            low = pl.multiple_of(zz * (16 * HD) + k * chunk, chunk)
-            acc[...] += dot(xbuf[:, pl.ds(low, chunk)], wv[pl.ds(low, chunk), :])
-            return carry
-
-        lax.fori_loop(0, 4, one, 0)
-
-    spread(0, lambda: None)
+            fillers[3 + shift]()
+
+        def finish():
+            for shift in range(4):
+                for eta in (0, 1):
+                    second[eta][shift][2]()
+
+        return finish
+
+    def project(zz, k):
+        t = zz * 16 + k * RING
+        part = jnp.concatenate([xbuf[t + j].reshape(BLOCK, HD) for j in range(RING)], axis=1)
+        acc[...] += dot(part, wv[pl.ds(pl.multiple_of(t * HD, RING * HD), RING * HD), :])
+
+    def idle():
+        pass
+
+    finish_own = spread(0, [idle] * 7)
     for one in load_w:
         one.wait()
-    z_block = xbuf.at[:, pl.ds(pl.multiple_of(z_partner * HD, HD), HD)]
+    z_block = xbuf.at[z_partner]
     remote(z_block, z_block, z_send, z_recv, head=z_partner).wait_recv()
-    spread(1, lambda: project(z))
-    project(1 - z)
+    steps = [lambda k=k: project(z, k) for k in range(RING)]
+    finish_other = spread(1, [finish_own, steps[0], steps[1], steps[2], steps[3], idle, idle])
+    finish_other()
+    for k in range(RING):
+        project(1 - z, k)
 
     def normalize(raw):
         return (raw * lax.rsqrt(jnp.mean(raw * raw, axis=-1, keepdims=True) + 1e-06)).astype(jnp.bfloat16)
@@ -448,7 +457,7 @@
         in_specs=[anywhere, anywhere, anywhere, vmem, vmem],
         out_specs=vmem,
         scratch_shapes=[
-            pltpu.VMEM((BLOCK, width), bf16),
+            pltpu.VMEM((width // HD, 2, HALF, HD), bf16),
             pltpu.VMEM((width, 3 * HD), bf16),
             pltpu.VMEM((HD, width), bf16),
             pltpu.VMEM((BLOCK, 3 * HD), f32),
@@ -483,7 +492,7 @@
             dma((2,)),
         ],
         compiler_params=pltpu.CompilerParams(collective_id=0, has_side_effects=True),
-    )(tokens, by_kind, out_weight, signs, rows)
+    )(tokens.reshape(2, HALF, HD), by_kind, out_weight, signs, rows)
 
 
 def solution(mesh):

time: 92.2 us -> 88.6 us (0.961)
  Pallas kernels: 90.5 us -> 87 us
    pallas_call x1, Pallas kernels: 90.5 us -> 87 us  [shards(): pl.pallas_call(kernel, out_shape=jax.ShapeDtypeStruct((BLOCK, HD), bf16),...]
where the time goes in v3:
time: 88.6 us; the launch traced here: 88.4 us
  Pallas kernels  87 us (98%)
  local copies, waits for them, and re-layouts  1.47 us (2%)
    pallas_call x1, Pallas kernels, shards(): pl.pallas_call(kernel, out_shape=jax.ShapeDtypeStruct((BLOCK, HD), bf16),...  87 us

profile of v3, /device:TPU:480, one launch (start us, length us, event | category | flops | bytes accessed | tf_op | source)
XLA Modules:
  0.0 88.4 jit_solution(1252118342897245608)
XLA Ops:
  0.0 87.0 %shard_map.55 = bf16[256,128]{1,0:T(8,128)(2,1)} custom-call(bf16[2,128,128]{2,1,0:T(8,128)(2,1)} %bitcast.3, bf16[3,4096,128]{2,1,0:T(8,128)(2,1)} %bitcast.2, bf16[128,4096]{1,0:T(8,128)(2,1)} %wo_ref.1, s32[1,2,128]{2,1,0:T(2,128)} %signs_ref.1, s32[1,2,64]{2,1,0:T(2,128)} %rows_ref.1), custom_call_target="tpu_custom_call" | custom-call | tf_op jit(solution)/shard_map/pallas_call | solution.py:454
  87.0 1.5 %copy.7 = bf16[256,128]{1,0:T(8,128)(2,1)} copy(bf16[256,128]{1,0:T(8,128)(2,1)} %shard_map.55) | data formatting | bytes 131072

commit v4 on v3

--- a/solution.py
+++ b/solution.py
@@ -12,6 +12,8 @@
 HALF = 128
 QUARTER = 64
 HD = 128
+NEAR = 32
+VIA = 1
 RING = 4
 SHIFTS = (0, 3, 1, 2)
 
@@ -131,23 +133,29 @@
             one.start()
             sent.append(one)
 
+        sides = ((3, 1), (1, 3), (2, 2))
+
         def start():
             send(0, piece(pos, 0, HALF), 1)
             send(1, piece(pos, 0, HALF), 3)
-
-        def relay(side):
-            if side == 0:
-                copy(0, piece(turn(pos, 3), 0, HALF), 1).wait_recv()
-                send(2, piece(turn(pos, 3), 0, QUARTER), 1)
-            else:
-                copy(1, piece(turn(pos, 1), 0, HALF), 3).wait_recv()
-                send(3, piece(turn(pos, 1), QUARTER, QUARTER), 3)
+            send(2, piece(pos, 0, HALF if phase == 0 else NEAR), 2)
+
+        def arrive(k):
+            low, goes = sides[k]
+            count = NEAR if phase == 1 and k == 2 else HALF
+            copy(k, piece(turn(pos, low), 0, count), goes).wait_recv()
+
+        def relay():
+            low, goes = sides[VIA]
+            arrive(VIA)
+            send(3, piece(turn(pos, low), NEAR, HALF - NEAR), goes)
 
         def finish():
-            copy(2, piece(turn(pos, 2), 0, QUARTER), 1).wait_recv()
-            copy(3, piece(turn(pos, 2), QUARTER, QUARTER), 3).wait_recv()
-
-        return start, relay, finish
+            arrive(1 - VIA)
+            arrive(2)
+            copy(3, piece(turn(pos, 2), NEAR, HALF - NEAR), sides[VIA][1]).wait_recv()
+
+        return start, arrive, relay, finish
 
     def spread(stage, fillers):
         first = [line(stage, eta, 0, 0) for eta in (0, 1)]
@@ -157,29 +165,20 @@
         for eta in (0, 1):
             second[eta][0][0]()
         fillers[0]()
-        for side in (0, 1):
+        for k in (0, 1, 2):
             for eta in (0, 1):
-                first[eta][1](side)
-                second[eta][1 + side][0]()
+                first[eta][1](k)
+                second[eta][1 + k][0]()
         fillers[1]()
-        for eta in (0, 1):
-            for side in (0, 1):
-                second[eta][0][1](side)
-        fillers[2]()
-        for eta in (0, 1):
-            first[eta][2]()
-            second[eta][3][0]()
-        fillers[3]()
-        for shift in (1, 2, 3):
-            for side in (0, 1):
-                for eta in (0, 1):
-                    second[eta][shift][1](side)
-            fillers[3 + shift]()
+        for shift in range(4):
+            for eta in (0, 1):
+                second[eta][shift][2]()
+            fillers[2 + shift]()
 
         def finish():
             for shift in range(4):
                 for eta in (0, 1):
-                    second[eta][shift][2]()
+                    second[eta][shift][3]()
 
         return finish
 
@@ -191,13 +190,13 @@
     def idle():
         pass
 
-    finish_own = spread(0, [idle] * 7)
+    finish_own = spread(0, [idle] * 6)
     for one in load_w:
         one.wait()
     z_block = xbuf.at[z_partner]
     remote(z_block, z_block, z_send, z_recv, head=z_partner).wait_recv()
     steps = [lambda k=k: project(z, k) for k in range(RING)]
-    finish_other = spread(1, [finish_own, steps[0], steps[1], steps[2], steps[3], idle, idle])
+    finish_other = spread(1, [finish_own, steps[0], steps[1], steps[2], steps[3], idle])
     finish_other()
     for k in range(RING):
         project(1 - z, k)
@@ -300,15 +299,18 @@
     attended = (num[...] / total).astype(jnp.bfloat16)
 
     load_wo.wait()
-    for stage in (0, 1):
+    def tiles(stage, rows):
         zz = 1 - z if stage == 0 else z
-        for row in range(RING):
+        for row in rows:
             low = pl.multiple_of((zz * 16 + row * RING) * HD, RING * HD)
             product = dot(attended, wov[:, pl.ds(low, RING * HD)]).astype(jnp.bfloat16)
             for col in range(RING):
                 tile = product[:, col * HD : (col + 1) * HD]
                 s1[0, stage, row, col] = tile[:HALF]
                 s1[1, stage, col, row] = tile[HALF:]
+
+    tiles(0, range(RING))
+    tiles(1, (0, 1))
 
     PAIR = RING // 2
 
@@ -351,11 +353,15 @@
         sent.append(one)
 
     ways = [(eta, side) for eta in (0, 1) for side in (0, 1)]
-    for stage in (0, 1):
+
+    def send_first(stage):
         for eta, side in ways:
             begin(rsa(stage, eta, side))
         for eta, side in ways:
             begin(rs1(stage, eta, side, 1 - side))
+
+    send_first(0)
+    tiles(1, (2, 3))
 
     f32 = jnp.float32
 
@@ -400,14 +406,13 @@
         return value
 
     relay_first(0)
+    send_first(1)
+    reduce_first(0)
     relay_first(1)
-    reduce_first(0)
     for eta in (0, 1):
         s3[eta] = reduce_second(0, eta).astype(jnp.bfloat16)
     for eta in (0, 1):
-        one = rs3(eta)
-        one.start()
-        sent.append(one)
+        begin(rs3(eta))
     reduce_first(1)
     for eta in (0, 1):
         t1[eta] = reduce_second(1, eta)

time: 88.6 us -> 85.2 us (0.962)
  the two profiles are of different devices: /device:TPU:480 before, /device:TPU:224 now
where the time goes in v4:
time: 85.2 us; the launch traced here: 85 us
  Pallas kernels  83.5 us (98%)
  local copies, waits for them, and re-layouts  1.47 us (2%)
    pallas_call x1, Pallas kernels, shards(): pl.pallas_call(kernel, out_shape=jax.ShapeDtypeStruct((BLOCK, HD), bf16),...  83.5 us

profile of v4, /device:TPU:224, one launch (start us, length us, event | category | flops | bytes accessed | tf_op | source)
XLA Modules:
  0.0 85.0 jit_solution(3743603042796196421)
XLA Ops:
  0.0 83.5 %shard_map.55 = bf16[256,128]{1,0:T(8,128)(2,1)} custom-call(bf16[2,128,128]{2,1,0:T(8,128)(2,1)} %bitcast.3, bf16[3,4096,128]{2,1,0:T(8,128)(2,1)} %bitcast.2, bf16[128,4096]{1,0:T(8,128)(2,1)} %wo_ref.1, s32[1,2,128]{2,1,0:T(2,128)} %signs_ref.1, s32[1,2,64]{2,1,0:T(2,128)} %rows_ref.1), custom_call_target="tpu_custom_call" | custom-call | tf_op jit(solution)/shard_map/pallas_call | solution.py:459
  83.6 1.5 %copy.7 = bf16[256,128]{1,0:T(8,128)(2,1)} copy(bf16[256,128]{1,0:T(8,128)(2,1)} %shard_map.55) | data formatting | bytes 131072

commit v5 on v4

--- a/solution.py
+++ b/solution.py
@@ -12,7 +12,7 @@
 HALF = 128
 QUARTER = 64
 HD = 128
-NEAR = 32
+NEAR = 64
 VIA = 1
 RING = 4
 SHIFTS = (0, 3, 1, 2)
@@ -182,10 +182,11 @@
 
         return finish
 
-    def project(zz, k):
+    def project(zz, k, low=0, high=3 * HD):
         t = zz * 16 + k * RING
         part = jnp.concatenate([xbuf[t + j].reshape(BLOCK, HD) for j in range(RING)], axis=1)
-        acc[...] += dot(part, wv[pl.ds(pl.multiple_of(t * HD, RING * HD), RING * HD), :])
+        deep = pl.ds(pl.multiple_of(t * HD, RING * HD), RING * HD)
+        acc[:, low:high] += dot(part, wv[deep, low:high])
 
     def idle():
         pass
@@ -199,7 +200,7 @@
     finish_other = spread(1, [finish_own, steps[0], steps[1], steps[2], steps[3], idle])
     finish_other()
     for k in range(RING):
-        project(1 - z, k)
+        project(1 - z, k, HD)
 
     def normalize(raw):
         return (raw * lax.rsqrt(jnp.mean(raw * raw, axis=-1, keepdims=True) + 1e-06)).astype(jnp.bfloat16)
@@ -218,34 +219,37 @@
     kvb[ctx, 0] = jnp.where(low_half, kf[:HALF], kf[HALF:]).astype(jnp.bfloat16)
     kvb[ctx, 1] = acc[:HALF, 2 * HD :].astype(jnp.bfloat16)
     kvb[ctx, 2] = acc[HALF:, 2 * HD :].astype(jnp.bfloat16)
+    for k in range(RING):
+        project(1 - z, k, 0, HD)
+
+    def kv(slot, piece, sems, target):
+        k = 3 * slot + piece
+        return remote(kvb.at[slot, piece], kvb.at[slot, piece], sems.at[k], kv_recv.at[k], ctx=target)
+
+    def up(slot):
+        return [kv(slot, piece, kv_send, ctx + 2) for piece in range(3)]
+
+    def over(slot):
+        return [kv(slot, piece, kv_pass, other_core) for piece in range(3)]
+
+    def values(slot):
+        return kvb[slot, pl.ds(1, 2)].reshape(BLOCK, HD)
+
+    @pl.when(zl < chips - 1)
+    def _():
+        for one in up(ctx):
+            one.start()
+
+    @pl.when(core == 0)
+    def _():
+        for one in over(ctx):
+            one.start()
+
     qn = normalize(acc[:, :HD])
     qd = twice(qn)
     lanes_low = lax.broadcasted_iota(jnp.int32, (BLOCK, HD), 1) < QUARTER
     qf[0] = jnp.where(lanes_low, qd, 0.0).astype(jnp.bfloat16)
     qf[1] = jnp.where(lanes_low, 0.0, qd).astype(jnp.bfloat16)
-
-    def kv(slot, piece, sems, target):
-        k = 3 * slot + piece
-        return remote(kvb.at[slot, piece], kvb.at[slot, piece], sems.at[k], kv_recv.at[k], ctx=target)
-
-    def up(slot):
-        return [kv(slot, piece, kv_send, ctx + 2) for piece in range(3)]
-
-    def over(slot):
-        return [kv(slot, piece, kv_pass, other_core) for piece in range(3)]
-
-    def values(slot):
-        return kvb[slot, pl.ds(1, 2)].reshape(BLOCK, HD)
-
-    @pl.when(zl < chips - 1)
-    def _():
-        for one in up(ctx):
-            one.start()
-
-    @pl.when(core == 0)
-    def _():
-        for one in over(ctx):
-            one.start()
 
     scores = dot_t(qn, kn)
     causal = (

time: 85.2 us -> 85 us (level)
  no operation moved by 1% of the time
where the time goes in v5:
time: 85 us; the launch traced here: 84.9 us
  Pallas kernels  83.4 us (98%)
  local copies, waits for them, and re-layouts  1.47 us (2%)
    pallas_call x1, Pallas kernels, shards(): pl.pallas_call(kernel, out_shape=jax.ShapeDtypeStruct((BLOCK, HD), bf16),...  83.4 us

profile of v5, /device:TPU:224, one launch (start us, length us, event | category | flops | bytes accessed | tf_op | source)
XLA Modules:
  0.0 84.9 jit_solution(3751161381787599942)
XLA Ops:
  0.0 83.4 %shard_map.55 = bf16[256,128]{1,0:T(8,128)(2,1)} custom-call(bf16[2,128,128]{2,1,0:T(8,128)(2,1)} %bitcast.3, bf16[3,4096,128]{2,1,0:T(8,128)(2,1)} %bitcast.2, bf16[128,4096]{1,0:T(8,128)(2,1)} %wo_ref.1, s32[1,2,128]{2,1,0:T(2,128)} %signs_ref.1, s32[1,2,64]{2,1,0:T(2,128)} %rows_ref.1), custom_call_target="tpu_custom_call" | custom-call | tf_op jit(solution)/shard_map/pallas_call | solution.py:463
  83.4 1.5 %copy.7 = bf16[256,128]{1,0:T(8,128)(2,1)} copy(bf16[256,128]{1,0:T(8,128)(2,1)} %shard_map.55) | data formatting | bytes 131072

commit v6 on v5

--- a/solution.py
+++ b/solution.py
@@ -272,6 +272,21 @@
         both = jnp.concatenate([left.astype(jnp.bfloat16), right.astype(jnp.bfloat16)], axis=1)
         num[...] += dot(both, values(slot))
 
+    def attend_pair(chip):
+        for one in over(2 * chip + 1 - core):
+            one.wait_recv()
+        packed = jnp.concatenate([kvb[2 * chip, 0], kvb[2 * chip + 1, 0]], axis=0)
+        left = dot_t(qf[0], packed)
+        right = dot_t(qf[1], packed)
+        left = left * left
+        right = right * right
+        wsum[...] += (left[:, :HD] + right[:, :HD]) + (left[:, HD:] + right[:, HD:])
+        left = left.astype(jnp.bfloat16)
+        right = right.astype(jnp.bfloat16)
+        both = jnp.concatenate([left[:, :HD], right[:, :HD], left[:, HD:], right[:, HD:]], axis=1)
+        pair = jnp.concatenate([values(2 * chip), values(2 * chip + 1)], axis=0)
+        num[...] += dot(both, pair)
+
     @pl.when(core == 1)
     def _():
         for one in over(2 * zl):
@@ -290,14 +305,17 @@
 
             kv(slot, piece, kv_pass, other_core).start()
 
-        attend(slot)
-        second = 2 * chip + 1 - core
-        for one in over(second):
-            one.wait_recv()
-        attend(second)
+        @pl.when(s > 0)
+        def _():
+            attend_pair(chip + 1)
+
         return carry
 
     lax.fori_loop(0, zl, earlier, 0)
+
+    @pl.when(zl > 0)
+    def _():
+        attend_pair(0)
 
     total = 1.0 + jnp.sum(wsum[...], axis=-1, keepdims=True)
     attended = (num[...] / total).astype(jnp.bfloat16)

time: 85 us -> 84 us (0.988)
  Pallas kernels: 83.4 us -> 82.4 us
    pallas_call x1, Pallas kernels: 83.4 us -> 82.4 us  [shards(): pl.pallas_call(kernel, out_shape=jax.ShapeDtypeStruct((BLOCK, HD), bf16),...]
where the time goes in v6:
time: 84 us; the launch traced here: 83.9 us
  Pallas kernels  82.4 us (98%)
  local copies, waits for them, and re-layouts  1.47 us (2%)
    pallas_call x1, Pallas kernels, shards(): pl.pallas_call(kernel, out_shape=jax.ShapeDtypeStruct((BLOCK, HD), bf16),...  82.4 us

profile of v6, /device:TPU:224, one launch (start us, length us, event | category | flops | bytes accessed | tf_op | source)
XLA Modules:
  0.0 83.9 jit_solution(9551562027558525198)
XLA Ops:
  0.0 82.4 %shard_map.55 = bf16[256,128]{1,0:T(8,128)(2,1)} custom-call(bf16[2,128,128]{2,1,0:T(8,128)(2,1)} %bitcast.3, bf16[3,4096,128]{2,1,0:T(8,128)(2,1)} %bitcast.2, bf16[128,4096]{1,0:T(8,128)(2,1)} %wo_ref.1, s32[1,2,128]{2,1,0:T(2,128)} %signs_ref.1, s32[1,2,64]{2,1,0:T(2,128)} %rows_ref.1), custom_call_target="tpu_custom_call" | custom-call | tf_op jit(solution)/shard_map/pallas_call | solution.py:481
  82.4 1.5 %copy.7 = bf16[256,128]{1,0:T(8,128)(2,1)} copy(bf16[256,128]{1,0:T(8,128)(2,1)} %shard_map.55) | data formatting | bytes 131072
